TPU v7x, 32 devices: a whole 2x2x4 slice. The times are simulated.
32 devices in a mesh: batch: 4 (over y, x), ctx: 8 (over z, core).
Axes of the slice: x: 2, y: 2, z: 4, core: 2. Of those that a mesh axis runs over, the one named last changes fastest.
Arguments:
- hidden: bfloat16 [4, 1024, 768], P('batch', 'ctx'), may hold values from -6 to 6
- cotangent: bfloat16 [4, 1024, 768], P('batch', 'ctx'), may hold values from -6 to 6
- w_qkv: bfloat16 [768, 2304], P(('batch', 'ctx')), may hold values from -3 to 3
- w_proj: bfloat16 [768, 768], P(('batch', 'ctx')), may hold values from -1.25 to 1.25
- w_inner: bfloat16 [768, 2304], P(('batch', 'ctx')), may hold values from -0.21875 to 0.21875
- w_down: bfloat16 [768, 1152], P(('batch', 'ctx')), may hold values from -0.1875 to 0.1875
- norm1_gain: bfloat16 [768], P(('batch', 'ctx')), may hold values from 0.5 to 1.5
- norm2_gain: bfloat16 [768], P(('batch', 'ctx')), may hold values from 0.5 to 1.5
Outputs:
- hidden_out: bfloat16 [4, 1024, 768], P('batch', 'ctx')
- hidden_grad: float32 [4, 1024, 768], P('batch', 'ctx')
- qkv_grad: float32 [768, 2304], P(('batch', 'ctx'))
- proj_grad: float32 [768, 768], P(('batch', 'ctx'))
- inner_grad: float32 [768, 2304], P(('batch', 'ctx'))
- down_grad: float32 [768, 1152], P(('batch', 'ctx'))
- norm1_grad: float32 [768], P(('batch', 'ctx'))
- norm2_grad: float32 [768], P(('batch', 'ctx'))
All inputs are finite; a program needn't handle non-finite values.
Results may differ from a plain program's by a relative error of at most 0.02.
Values may be sent and summed in bfloat16 or wider, within the bound.
A program may use at most 192 MiB of HBM per device.

v0:
```python
import jax
import jax.numpy as jnp
from jax import lax
from jax.sharding import PartitionSpec as P

D = 768
HEADS = 12
HEAD_DIM = 64
FF = 1152


norm_eps = 1e-05
rope_base = 160000.0


def apply_layer_norm(values, gain_vector):
    centre = jnp.mean(values, axis=-1, keepdims=True)
    shifted = values - centre
    spread = jnp.mean(shifted * shifted, axis=-1, keepdims=True)
    inverse = lax.rsqrt(spread + norm_eps)
    normed = shifted * inverse
    return (normed * gain_vector, normed, inverse)


def layer_norm_gradient(upstream, gain_vector, normed, inverse):
    scaled = upstream * gain_vector
    first_mean = jnp.mean(scaled, axis=-1, keepdims=True)
    second_mean = jnp.mean(scaled * normed, axis=-1, keepdims=True)
    return (
        inverse * (scaled - first_mean - normed * second_mean),
        jnp.sum(upstream * normed, axis=0),
    )


def rope_tables(offset, row_count, head_width):
    half_dim = head_width // 2
    position = (offset + jnp.arange(row_count, dtype=jnp.int32)).astype(jnp.float32)
    exponent = jnp.arange(half_dim, dtype=jnp.int32).astype(jnp.float32) * (-2.0 / head_width)
    angles = position[:, None] * jnp.power(rope_base, exponent)[None, :]
    return (jnp.cos(angles), jnp.sin(angles))


def rotate(values, cosine, sine_table, direction):
    half_dim = values.shape[-1] // 2
    front_half = values[..., :half_dim]
    back_half = values[..., half_dim:]
    cos_rows = cosine[:, None, :]
    sin_rows = sine_table[:, None, :] * direction
    return jnp.concatenate(
        [
            front_half * cos_rows - back_half * sin_rows,
            back_half * cos_rows + front_half * sin_rows,
        ],
        axis=-1,
    )


def gelu_parts(act_input):
    normal_cdf = 0.5 * (1.0 + jax.scipy.special.erf(act_input * 0.7071067811865476))
    density = jnp.exp(-0.5 * act_input * act_input) * 0.3989422804014327
    return (act_input * normal_cdf, normal_cdf + act_input * density)


def as_heads(flat_rows):
    return flat_rows.reshape(flat_rows.shape[0], HEADS, HEAD_DIM)


def pair_terms(query_rows, grad_rows, log_rows, delta_rows, key_rows, value_rows, score_scale):
    scores = (
        jnp.einsum("qhd,khd->hqk", query_rows, key_rows, preferred_element_type=jnp.float32)
        * score_scale
    )
    probabilities = jnp.exp(scores - log_rows[..., None])
    grad_dots = jnp.einsum(
        "qhd,khd->hqk", grad_rows, value_rows, preferred_element_type=jnp.float32
    )
    dscore = (probabilities * (grad_dots - delta_rows[..., None])).astype(jnp.bfloat16)
    return (probabilities.astype(jnp.bfloat16), dscore)


def local(hidden, cotangent, w_qkv, w_proj, w_inner, w_down, norm1_gain, norm2_gain):
    token_rows = hidden.shape[1]
    score_scale = HEAD_DIM ** (-0.5)
    full_qkv, full_proj, full_inner, full_down, gain_first, gain_second = (
        lax.all_gather(w_qkv, ("batch", "ctx"), axis=0, tiled=True),
        lax.all_gather(w_proj, ("batch", "ctx"), axis=0, tiled=True),
        lax.all_gather(w_inner, ("batch", "ctx"), axis=0, tiled=True),
        lax.all_gather(w_down, ("batch", "ctx"), axis=0, tiled=True),
        lax.all_gather(norm1_gain, ("batch", "ctx"), axis=0, tiled=True),
        lax.all_gather(norm2_gain, ("batch", "ctx"), axis=0, tiled=True),
    )
    first_norm_gain = gain_first.astype(jnp.float32)
    second_norm_gain = gain_second.astype(jnp.float32)
    input_tokens = hidden[0].astype(jnp.float32)
    first_normed_rows, first_centered_rows, first_inverse_deviation = apply_layer_norm(
        input_tokens, first_norm_gain
    )
    h_one = first_normed_rows.astype(jnp.bfloat16)
    projected = jnp.dot(h_one, full_qkv, preferred_element_type=jnp.float32)
    cosine, sine_table = rope_tables(lax.axis_index("ctx") * token_rows, token_rows, HEAD_DIM)
    query_rot = rotate(as_heads(projected[:, :D]), cosine, sine_table, 1.0).astype(jnp.bfloat16)
    key_flat = (
        rotate(as_heads(projected[:, D : 2 * D]), cosine, sine_table, 1.0)
        .astype(jnp.bfloat16)
        .reshape(token_rows, D)
    )
    value_flat = projected[:, 2 * D :].astype(jnp.bfloat16)
    key_rot = as_heads(key_flat)
    value_rows = as_heads(value_flat)
    zero_heads = jnp.zeros((token_rows, HEADS, HEAD_DIM), jnp.float32)
    piece_rows = (
        lax.all_gather(key_flat, "ctx", axis=0, tiled=True),
        lax.all_gather(value_flat, "ctx", axis=0, tiled=True),
    )
    row_peak = jnp.full((HEADS, token_rows), -jnp.inf, jnp.float32)
    row_total = jnp.zeros((HEADS, token_rows), jnp.float32)
    key_piece = as_heads(piece_rows[0])
    value_piece = as_heads(piece_rows[1])
    scores = (
        jnp.einsum("qhd,khd->hqk", query_rot, key_piece, preferred_element_type=jnp.float32)
        * score_scale
    )
    new_peak = jnp.max(scores, axis=-1)
    row_fade = jnp.exp(row_peak - new_peak)
    probabilities = jnp.exp(scores - new_peak[..., None])
    new_total = row_total * row_fade + jnp.sum(probabilities, axis=-1)
    new_mixture = zero_heads * jnp.transpose(row_fade)[:, :, None] + jnp.einsum(
        "hqk,khd->qhd",
        probabilities.astype(jnp.bfloat16),
        value_piece,
        preferred_element_type=jnp.float32,
    )
    log_total = new_peak + jnp.log(new_total)
    attended = (
        (new_mixture / jnp.transpose(new_total)[:, :, None])
        .reshape(token_rows, D)
        .astype(jnp.bfloat16)
    )
    residual_stream = input_tokens + jnp.dot(
        attended, full_proj, preferred_element_type=jnp.float32
    )
    second_normed_rows, second_centered_rows, second_inverse_deviation = apply_layer_norm(
        residual_stream, second_norm_gain
    )
    h_two = second_normed_rows.astype(jnp.bfloat16)
    inner_all = jnp.dot(h_two, full_inner, preferred_element_type=jnp.float32)
    act_half = inner_all[:, :FF]
    gate_half = inner_all[:, FF:]
    activated, gelu_slope = gelu_parts(act_half)
    middle = (activated * gate_half).astype(jnp.bfloat16)
    output_rows = residual_stream + jnp.einsum(
        "tf,df->td", middle, full_down, preferred_element_type=jnp.float32
    )
    back_qkv, back_proj, back_inner, back_down = (full_qkv, full_proj, full_inner, full_down)
    upstream = cotangent[0]
    d_middle = jnp.dot(upstream, back_down, preferred_element_type=jnp.float32)
    d_inner = jnp.concatenate(
        [d_middle * gate_half * gelu_slope, d_middle * activated], axis=-1
    ).astype(jnp.bfloat16)
    second_hidden_gradient = jnp.einsum(
        "te,de->td", d_inner, back_inner, preferred_element_type=jnp.float32
    )
    residual_norm_gradient, second_gain_portion = layer_norm_gradient(
        second_hidden_gradient, second_norm_gain, second_centered_rows, second_inverse_deviation
    )
    d_resid = upstream.astype(jnp.float32) + residual_norm_gradient
    d_resid_low = d_resid.astype(jnp.bfloat16)
    d_attended = jnp.einsum(
        "td,ed->te", d_resid_low, back_proj, preferred_element_type=jnp.float32
    ).astype(jnp.bfloat16)
    grad_heads = as_heads(d_attended)
    row_delta = jnp.transpose(
        jnp.sum(grad_heads.astype(jnp.float32) * as_heads(attended).astype(jnp.float32), axis=-1)
    )
    log_whole, delta_whole = (
        lax.all_gather(log_total, "ctx", axis=1, tiled=True),
        lax.all_gather(row_delta, "ctx", axis=1, tiled=True),
    )
    piece_rows = (
        lax.all_gather(key_flat, "ctx", axis=0, tiled=True),
        lax.all_gather(value_flat, "ctx", axis=0, tiled=True),
    )
    key_part = as_heads(piece_rows[0])
    value_part = as_heads(piece_rows[1])
    probs_low, dscore = pair_terms(
        query_rot, grad_heads, log_total, row_delta, key_part, value_part, score_scale
    )
    query_grad = (
        jnp.einsum("hqk,khd->qhd", dscore, key_part, preferred_element_type=jnp.float32)
        * score_scale
    )
    piece_rows = (
        lax.all_gather(query_rot.reshape(token_rows, D), "ctx", axis=0, tiled=True),
        lax.all_gather(d_attended, "ctx", axis=0, tiled=True),
    )
    query_part = as_heads(piece_rows[0])
    grad_part = as_heads(piece_rows[1])
    probs_low, dscore = pair_terms(
        query_part, grad_part, log_whole, delta_whole, key_rot, value_rows, score_scale
    )
    key_sum = (
        jnp.einsum("hqk,qhd->khd", dscore, query_part, preferred_element_type=jnp.float32)
        * score_scale
    )
    value_sum = jnp.einsum("hqk,qhd->khd", probs_low, grad_part, preferred_element_type=jnp.float32)
    d_query = rotate(query_grad, cosine, sine_table, -1.0)
    d_key = rotate(key_sum, cosine, sine_table, -1.0)
    d_projected = jnp.concatenate(
        [
            d_query.reshape(token_rows, D),
            d_key.reshape(token_rows, D),
            value_sum.reshape(token_rows, D),
        ],
        axis=-1,
    ).astype(jnp.bfloat16)
    first_hidden_gradient = jnp.einsum(
        "te,de->td", d_projected, back_qkv, preferred_element_type=jnp.float32
    )
    input_norm_gradient, first_gain_portion = layer_norm_gradient(
        first_hidden_gradient, first_norm_gain, first_centered_rows, first_inverse_deviation
    )
    input_grad = d_resid + input_norm_gradient

    def grad_rows(start, count):
        return jnp.concatenate(
            [
                jnp.einsum("td,te->de", h_one, d_projected, preferred_element_type=jnp.float32),
                jnp.einsum("te,td->ed", attended, d_resid_low, preferred_element_type=jnp.float32),
                jnp.einsum("td,te->de", h_two, d_inner, preferred_element_type=jnp.float32),
                jnp.einsum("td,tf->df", upstream, middle, preferred_element_type=jnp.float32),
                first_gain_portion[:, None],
                second_gain_portion[:, None],
            ],
            axis=1,
        )

    owned_rows = D // lax.axis_size(("batch", "ctx"))
    grad_share = lax.psum_scatter(
        grad_rows(jnp.int32(0), owned_rows * lax.axis_size(("batch", "ctx"))),
        ("batch", "ctx"),
        scatter_dimension=0,
        tiled=True,
    )
    qkv_share = grad_share[:, : 3 * D]
    proj_share = grad_share[:, 3 * D : 4 * D]
    inner_share = grad_share[:, 4 * D : 4 * D + 2 * FF]
    down_share = grad_share[:, 4 * D + 2 * FF : 4 * D + 3 * FF]
    first_share = grad_share[:, 4 * D + 3 * FF]
    second_share = grad_share[:, 4 * D + 3 * FF + 1]
    return (
        output_rows.astype(jnp.bfloat16)[None],
        input_grad[None],
        qkv_share,
        proj_share,
        inner_share,
        down_share,
        first_share,
        second_share,
    )


def solution(mesh):
    placed = (
        P("batch", "ctx", None),
        P("batch", "ctx", None),
        P(("batch", "ctx"), None),
        P(("batch", "ctx"), None),
        P(("batch", "ctx"), None),
        P(("batch", "ctx"), None),
        P(("batch", "ctx")),
        P(("batch", "ctx")),
    )
    return jax.shard_map(
        local,
        mesh=mesh,
        in_specs=placed,
        out_specs=(
            P("batch", "ctx", None),
            P("batch", "ctx", None),
            P(("batch", "ctx"), None),
            P(("batch", "ctx"), None),
            P(("batch", "ctx"), None),
            P(("batch", "ctx"), None),
            P(("batch", "ctx")),
            P(("batch", "ctx")),
        ),
        check_vma=False,
    )
```

profile of v0, /device:TPU:0, one launch (start us, length us, event | category | flops | bytes accessed | tf_op | source)
XLA Modules:
  0.0 641.2 jit_solution(14519602445404281982)
XLA Ops:
  7.2 0.7 all-gather.9.cloned.1.call-update
  8.0 0.8 dynamic-update-slice
  8.8 0.8 dynamic-update-slice.1
  9.6 42.2 %all-reduce.2 = (bf16[768]{0:T(1024)(128)(2,1)S(1)}, bf16[768]{0:T(1024)(128)(2,1)S(1)}) all-reduce(bf16[768]{0:T(1024)(128)(2,1)S(1)} %dynamic-update-slice, bf16[768]{0:T(1024)(128)(2,1)S(1)} %dynamic-update-slice.1), channel_id=1, replica_groups=mesh['batch'=4,'ctx'=8] {'batch','ctx'}, use_global_device_ids=true, to_apply=%add | all-reduce | flops 1536 | bytes 6144
  51.9 1.0 convert_reduce_fusion
  52.9 1.1 fusion.58
  54.1 0.8 broadcast_multiply_fusion
  54.8 19.1 %all-gather.9.cloned.1.call-done = bf16[768,2304]{1,0:T(8,128)(2,1)} async-done(((bf16[24,2304]{1,0:T(8,128)(2,1)}), bf16[768,2304]{1,0:T(8,128)(2,1)}) %all-gather.9.cloned.1.call-update) | async-done | bytes 3538960 | tf_op jit(solution)/shard_map/all_gather | solution.py:85
  73.9 2.8 fusion.79
  76.8 0.2 copy.26
  77.0 0.2 copy.25
  77.2 0.1 multiply_subtract_fusion
  77.3 0.6 copy-done.9
  77.9 0.7 maximum_convert_fusion.1
  78.7 0.7 slice.134
  79.5 0.5 all-gather.15.cloned.1.call-update
  80.0 0.5 all-gather.17.cloned.1.call-update
  80.6 0.5 all-gather.19.cloned.1.call-update
  81.2 0.7 maximum_convert_fusion
  82.0 22.7 %all-gather.11.cloned.1.call-done = bf16[1024,768]{0,1:T(8,128)(2,1)} async-done(((bf16[128,768]{0,1:T(8,128)(2,1)}), bf16[1024,768]{0,1:T(8,128)(2,1)}) %all-gather.11.cloned.1.call-update) | async-done | bytes 1572880 | tf_op jit(solution)/shard_map/all_gather | solution.py:112
  104.7 2.5 multiply_reduce_fusion
  107.2 1.3 fusion
  108.5 1.4 copy-done
  109.9 21.1 %all-gather.13.cloned.1.call-done = bf16[1024,768]{1,0:T(8,128)(2,1)} async-done(((bf16[128,768]{1,0:T(8,128)(2,1)}), bf16[1024,768]{1,0:T(8,128)(2,1)}) %all-gather.13.cloned.1.call-update) | async-done | bytes 1572880 | tf_op jit(solution)/shard_map/all_gather | solution.py:113
  131.0 1.7 copy.27
  132.7 4.8 fusion.35
  137.5 49.6 %all-gather.15.cloned.1.call-done = bf16[768,768]{1,0:T(8,128)(2,1)} async-done(((bf16[24,768]{1,0:T(8,128)(2,1)}), bf16[768,768]{1,0:T(8,128)(2,1)}) %all-gather.15.cloned.1.call-update) | async-done | bytes 1179664 | tf_op jit(solution)/shard_map/all_gather | solution.py:86
  187.1 1.7 fusion.84
  188.9 0.2 multiply_reduce_fusion.4
  189.1 59.9 %all-gather.17.cloned.1.call-done = bf16[768,2304]{1,0:T(8,128)(2,1)} async-done(((bf16[24,2304]{1,0:T(8,128)(2,1)}), bf16[768,2304]{1,0:T(8,128)(2,1)}) %all-gather.17.cloned.1.call-update) | async-done | bytes 3538960 | tf_op jit(solution)/shard_map/all_gather | solution.py:87
  249.0 2.7 fusion.81
  251.6 54.4 %all-gather.19.cloned.1.call-done = bf16[768,1152]{1,0:T(8,128)(2,1)} async-done(((bf16[24,1152]{1,0:T(8,128)(2,1)}), bf16[768,1152]{1,0:T(8,128)(2,1)}) %all-gather.19.cloned.1.call-update) | async-done | bytes 1769488 | tf_op jit(solution)/shard_map/all_gather | solution.py:88
  306.1 2.2 fusion.43
  308.3 0.3 copy-done.5
  308.6 1.4 multiply_reduce_fusion.1
  310.1 0.2 multiply_add_fusion
  310.3 1.2 convolution_convert_fusion
  311.6 0.8 copy.30
  312.4 1.1 copy.28
  313.5 0.9 broadcast_in_dim.19
  314.4 15.1 %all_gather.47 = f32[12,1024]{1,0:T(8,128)} all-gather(f32[12,128]{1,0:T(8,128)S(1)} %get-tuple-element.36), channel_id=1, replica_groups=mesh['batch'=4,'ctx'=8] {'ctx'}, dimensions={1}, use_global_device_ids=true | all-gather | bytes 55296 | tf_op jit(solution)/shard_map/all_gather | solution.py:176
  329.5 0.1 multiply_reduce_fusion.2
  329.6 15.2 %all_gather.49 = f32[12,1024]{1,0:T(8,128)} all-gather(f32[12,128]{1,0:T(8,128)S(1)} %bitcast.128), channel_id=1, replica_groups=mesh['batch'=4,'ctx'=8] {'ctx'}, dimensions={1}, use_global_device_ids=true | all-gather | bytes 55296 | tf_op jit(solution)/shard_map/all_gather | solution.py:177
  344.8 0.4 fusion.66
  345.3 3.8 convolution_bitcast_fusion
  349.1 4.1 fusion.59
  353.2 5.1 fusion.85
  358.4 7.3 %fusion.23 = f32[128,12,64]{0,2,1:T(8,128)} fusion(bf16[1024,12,64]{0,2,1:T(8,128)(2,1)} %bitcast.114, f32[12,128,1024]{2,1,0:T(8,128)} %copy-done, f32[12,128]{1,0:T(8,128)S(1)} %bitcast.129, f32[12,128]{1,0:T(8,128)} %copy-done.21, bf16[128,12,64]{0,2,1:T(8,128)(2,1)} %bitcast.120, bf16[1024,12,64]{0,2,1:T(8,128)(2,1)} %bitcast.110), kind=kOutput, calls=%fused_computation.25 | convolution fusion | flops 410615808 | bytes 10039296 | tf_op jit(solution)/shard_map/hqk,khd->qhd/dot_general | solution.py:189
  365.6 2.6 copy.29
  368.2 4.5 fusion.28
  372.7 8.9 %fusion.21 = f32[128,12,64]{0,2,1:T(8,128)} fusion(bf16[1024,12,64]{0,2,1:T(8,128)(2,1)} %bitcast.116, f32[12,1024,128]{2,1,0:T(8,128)} %fusion.85, f32[12,1024]{1,0:T(8,128)} %all_gather.49, f32[12,1024]{1,0:T(8,128)} %all_gather.47, bf16[1024,12,64]{0,2,1:T(8,128)(2,1)} %bitcast.106, bf16[128,12,64]{0,2,1:T(8,128)(2,1)} %bitcast.127), kind=kOutput, calls=%fused_computation.23 | convolution fusion | flops 410615808 | bytes 10125312 | tf_op jit(solution)/shard_map/hqk,qhd->khd/dot_general | solution.py:202
  381.6 1.4 subtract_convert_fusion.1
  383.0 4.1 fusion.61
  387.1 2.6 fusion.57
  389.7 0.9 broadcast_in_dim.18
  390.6 22.2 %concatenate.31 = f32[768,6530]{1,0:T(8,128)} concatenate(f32[768,2304]{1,0:T(8,128)} %fusion.61, f32[768,768]{1,0:T(8,128)S(1)} %fusion.66, f32[768,2304]{1,0:T(8,128)} %fusion.59, f32[768,1152]{1,0:T(8,128)} %convolution_bitcast_fusion, f32[768,1]{1,0:T(8,128)} %broadcast_in_dim.18, f32[768,1]{1,0:T(8,128)} %broadcast_in_dim.19), dimensions={1} | concatenate | bytes 40120320 | tf_op jit(solution)/shard_map/concatenate | solution.py:225
  412.9 1.2 copy-done.4
  414.1 2.9 fusion.31
  417.0 0.9 fusion.56
  417.9 210.3 %reduce-scatter.2.cloned.1.call-done = f32[24,6530]{1,0:T(8,128)} async-done(((f32[768,6530]{1,0:T(8,128)}), f32[24,6530]{1,0:T(8,128)}) %reduce-scatter.2.cloned.1.call-update) | async-done | bytes 626896 | tf_op jit(solution)/shard_map/reduce_scatter | solution.py:238
  628.3 1.5 slice_reduce_fusion
  629.7 1.5 slice.91
  631.3 1.5 slice.93
  632.8 1.8 fusion.83
  (92 shorter events, 0.7 us)
Async XLA Ops:
  7.2 66.8 %all-gather.9.cloned.1.call-start = ((), (), s32[]{:S(2)}) async-start(), calls=%async_computation.1 | async-start | bytes 3649536 | tf_op jit(solution)/shard_map/all_gather | solution.py:85
  7.9 96.8 %all-gather.11.cloned.1.call-start = ((), (), s32[]{:S(2)}) async-start(), calls=%async_computation.2 | async-start | bytes 1769472 | tf_op jit(solution)/shard_map/all_gather | solution.py:112
  52.9 23.9 %copy-start.22 = (f32[128]{0:T(128)}, f32[128]{0:T(128)S(1)}, u32[]{:S(2)}) copy-start(f32[128]{0:T(128)S(1)} %broadcast_multiply_fusion.6) | copy-start | bytes 1540
  54.1 22.7 %copy-start.26 = (f32[128]{0:T(128)}, f32[128]{0:T(128)S(1)}, u32[]{:S(2)}) copy-start(f32[128]{0:T(128)S(1)} %add_rsqrt_fusion.1) | copy-start | bytes 1540
  54.8 22.3 %copy-start.20 = (f32[128,32]{0,1:T(8,128)}, f32[128,32]{0,1:T(8,128)S(1)}, u32[]{:S(2)}) copy-start(f32[128,32]{0,1:T(8,128)S(1)} %get-tuple-element.40) | copy-start | bytes 49156
  77.3 0.6 copy-start.9
  77.3 1.3 copy-start.11
  78.6 52.3 %all-gather.13.cloned.1.call-start = ((), (), s32[]{:S(2)}) async-start(), calls=%async_computation.3 | async-start | bytes 1769472 | tf_op jit(solution)/shard_map/all_gather | solution.py:113
  79.4 107.7 %all-gather.15.cloned.1.call-start = ((), (), s32[]{:S(2)}) async-start(), calls=%async_computation.4 | async-start | bytes 1216512 | tf_op jit(solution)/shard_map/all_gather | solution.py:86
  80.0 169.0 %all-gather.17.cloned.1.call-start = ((), (), s32[]{:S(2)}) async-start(), calls=%async_computation.5 | async-start | bytes 3649536 | tf_op jit(solution)/shard_map/all_gather | solution.py:87
  80.6 225.5 %all-gather.19.cloned.1.call-start = ((), (), s32[]{:S(2)}) async-start(), calls=%async_computation.6 | async-start | bytes 1824768 | tf_op jit(solution)/shard_map/all_gather | solution.py:88
  81.2 272.1 %all-gather.21.cloned.1.call-start = ((), (), s32[]{:S(2)}) async-start(), calls=%async_computation.7 | async-start | bytes 1769472 | tf_op jit(solution)/shard_map/all_gather | solution.py:193
  81.9 283.7 %all-gather.23.cloned.1.call-start = ((), (), s32[]{:S(2)}) async-start(), calls=%async_computation.8 | async-start | bytes 1769472 | tf_op jit(solution)/shard_map/all_gather | solution.py:194
  107.2 2.7 copy-start
  109.9 204.6 %copy-start.21 = (f32[12,128]{1,0:T(8,128)}, f32[12,128]{1,0:T(8,128)S(1)}, u32[]{:S(2)}) copy-start(f32[12,128]{1,0:T(8,128)S(1)} %get-tuple-element.36) | copy-start | bytes 18436
  132.7 4.8 copy-start.8
  132.7 54.4 %copy-start.1 = (bf16[1,128,768]{2,1,0:T(8,128)(2,1)S(1)}, bf16[1,128,768]{2,1,0:T(8,128)(2,1)}, u32[]{:S(2)}) copy-start(bf16[1,128,768]{2,1,0:T(8,128)(2,1)} %param.8) | copy-start | bytes 589828
  188.9 117.2 %copy-start.13 = (bf16[1,128,768]{2,1,0:T(8,128)(2,1)S(1)}, bf16[1,128,768]{2,1,0:T(8,128)(2,1)}, u32[]{:S(2)}) copy-start(bf16[1,128,768]{2,1,0:T(8,128)(2,1)} %param.9) | copy-start | bytes 589828
  188.9 121.2 %copy-start.24 = (f32[128]{0:T(128)}, f32[128]{0:T(128)S(1)}, u32[]{:S(2)}) copy-start(f32[128]{0:T(128)S(1)} %broadcast_multiply_fusion.5) | copy-start | bytes 1540
  189.1 121.0 %copy-start.28 = (f32[128]{0:T(128)}, f32[128]{0:T(128)S(1)}, u32[]{:S(2)}) copy-start(f32[128]{0:T(128)S(1)} %add_rsqrt_fusion) | copy-start | bytes 1540
  251.6 56.7 %copy-start.3 = (f32[128,2304]{1,0:T(8,128)}, f32[128,2304]{1,0:T(8,128)S(1)}, u32[]{:S(2)}) copy-start(f32[128,2304]{1,0:T(8,128)S(1)} %fusion.81) | copy-start | bytes 3538948
  306.1 2.5 copy-start.5
  308.3 1.7 copy-start.18
  308.3 2.0 copy-start.16
  308.6 1.7 copy-start.2
  308.6 3.0 copy-start.7
  311.5 316.7 %reduce-scatter.2.cloned.1.call-start = ((), (), s32[]{:S(2)}) async-start(), calls=%async_computation.9 | async-start | bytes 21086208 | tf_op jit(solution)/shard_map/reduce_scatter | solution.py:238
  313.5 16.1 %copy-start.14 = (bf16[128,768]{0,1:T(8,128)(2,1)}, bf16[128,768]{0,1:T(8,128)(2,1)S(1)}, u32[]{:S(2)}) copy-start(bf16[128,768]{0,1:T(8,128)(2,1)S(1)} %copy.28) | copy-start | bytes 589828
  344.8 4.2 copy-start.17
  344.8 4.2 copy-start.19
  344.8 4.2 copy-start.25
  344.8 4.2 copy-start.29
  349.1 4.2 copy-start.10
  349.1 4.1 copy-start.12
  372.7 10.3 %copy-start.23 = (f32[128]{0:T(128)S(1)}, f32[128]{0:T(128)}, u32[]{:S(2)}) copy-start(f32[128]{0:T(128)} %copy-done.22) | copy-start | bytes 1540
  372.7 10.3 %copy-start.27 = (f32[128]{0:T(128)S(1)}, f32[128]{0:T(128)}, u32[]{:S(2)}) copy-start(f32[128]{0:T(128)} %copy-done.26) | copy-start | bytes 1540
  383.0 4.1 copy-start.6
  412.8 1.3 copy-start.4
  412.8 4.2 copy-start.30
  414.1 2.9 copy-start.15
Sparse Core Ops, SparseCore 0:
  11.0 62.9 all-gather.8
  78.8 25.8 all-gather.10
  106.9 24.0 all-gather.12
  133.9 53.2 all-gather.14
  190.0 58.9 all-gather.16
  251.7 54.3 all-gather.18
  308.2 26.2 all-gather.20
  336.8 24.9 all-gather.22
  413.0 215.2 reduce-scatter.1
where the time goes:
time: 642 us; the launch traced here: 641 us
  waiting for transfers between devices  439 us (68%)
  blocking collectives  72.5 us (11%)
  matrix products  62.9 us (10%)
  local copies, waits for them, and re-layouts  43 us (7%)
  between operations  14.3 us (2%)
  other arithmetic  8.55 us (1%)
    reduce_scatter x1, waiting for transfers between devices, local(): lax.psum_scatter(grad_rows(jnp.int32(0), owned_rows * lax.axis_size(('bat...  210 us
    all_gather x1, waiting for transfers between devices, local(): lax.all_gather(w_inner, ('batch', 'ctx'), axis=0, tiled=True)  59.9 us
    all_gather x1, waiting for transfers between devices, local(): lax.all_gather(w_down, ('batch', 'ctx'), axis=0, tiled=True)  54.4 us
    all_gather x1, waiting for transfers between devices, local(): lax.all_gather(w_proj, ('batch', 'ctx'), axis=0, tiled=True)  49.6 us
    unnamed x1, blocking collectives  42.2 us
    all_gather x1, waiting for transfers between devices, local(): lax.all_gather(key_flat, 'ctx', axis=0, tiled=True)  22.7 us
    concatenate x1, local copies, waits for them, and re-layouts, grad_rows(): jnp.concatenate([jnp.einsum('td,te->de', h_one, d_projected, preferred_el...  22.2 us
    all_gather x1, waiting for transfers between devices, local(): lax.all_gather(value_flat, 'ctx', axis=0, tiled=True)  21.1 us
  transfers between devices with their start and end apart: 9, of which 7 were waited for; matrix products, arithmetic and copies ran while one was open for 8% of the time, Pallas kernels for 0%

commit v1 on v0

v1 whole, which is shorter than its diff:
```python
import functools
import math

import jax
import jax.numpy as jnp
from jax import lax
from jax.experimental import pallas as pl
from jax.experimental.pallas import tpu as pltpu
from jax.sharding import PartitionSpec as P

D = 768
HEADS = 12
HEAD_DIM = 64
FF = 1152


norm_eps = 1e-05
rope_base = 160000.0


def apply_layer_norm(values, gain_vector):
    centre = jnp.mean(values, axis=-1, keepdims=True)
    shifted = values - centre
    spread = jnp.mean(shifted * shifted, axis=-1, keepdims=True)
    inverse = lax.rsqrt(spread + norm_eps)
    normed = shifted * inverse
    return (normed * gain_vector, normed, inverse)


def layer_norm_gradient(upstream, gain_vector, normed, inverse):
    scaled = upstream * gain_vector
    first_mean = jnp.mean(scaled, axis=-1, keepdims=True)
    second_mean = jnp.mean(scaled * normed, axis=-1, keepdims=True)
    return (
        inverse * (scaled - first_mean - normed * second_mean),
        jnp.sum(upstream * normed, axis=0),
    )


def rope_tables(offset, row_count, head_width):
    half_dim = head_width // 2
    position = (offset + jnp.arange(row_count, dtype=jnp.int32)).astype(jnp.float32)
    exponent = jnp.arange(half_dim, dtype=jnp.int32).astype(jnp.float32) * (-2.0 / head_width)
    angles = position[:, None] * jnp.power(rope_base, exponent)[None, :]
    return (jnp.cos(angles), jnp.sin(angles))


def rotate(values, cosine, sine_table, direction):
    half_dim = values.shape[-1] // 2
    front_half = values[..., :half_dim]
    back_half = values[..., half_dim:]
    cos_rows = cosine[:, None, :]
    sin_rows = sine_table[:, None, :] * direction
    return jnp.concatenate(
        [
            front_half * cos_rows - back_half * sin_rows,
            back_half * cos_rows + front_half * sin_rows,
        ],
        axis=-1,
    )


def gelu_parts(act_input):
    normal_cdf = 0.5 * (1.0 + jax.scipy.special.erf(act_input * 0.7071067811865476))
    density = jnp.exp(-0.5 * act_input * act_input) * 0.3989422804014327
    return (act_input * normal_cdf, normal_cdf + act_input * density)


def as_heads(flat_rows):
    return flat_rows.reshape(flat_rows.shape[0], HEADS, HEAD_DIM)


EVERY = ("batch", "ctx")
LANES = 128


def weight_grad_kernel(bounds, *refs):
    count = len(bounds) - 1
    lefts, rights, gains_ref, out_ref = refs[:count], refs[count : 2 * count], refs[-2], refs[-1]
    step = pl.program_id(0)
    for index in range(count):

        @pl.when(jnp.logical_and(step >= bounds[index], step < bounds[index + 1]))
        def _(left=lefts[index], right=rights[index]):
            out_ref[...] = lax.dot_general(
                left[...],
                right[...],
                (((0,), (0,)), ((), ())),
                preferred_element_type=jnp.float32,
            ).astype(out_ref.dtype)

    @pl.when(step == bounds[count])
    def _():
        out_ref[:, :LANES] = gains_ref[...].astype(out_ref.dtype)


def weight_grads(pairs, gain_columns):
    rows, width = pairs[0][0].shape
    widths = [right.shape[1] for _, right in pairs]
    block = math.gcd(*widths)
    bounds = [0]
    for part in widths:
        bounds.append(bounds[-1] + part // block)

    def right_index(start, count, step):
        return (0, jnp.clip(step - start, 0, count - 1))

    whole = lambda step: (0, 0)
    total = sum(widths) + LANES
    return pl.pallas_call(
        functools.partial(weight_grad_kernel, tuple(bounds)),
        out_shape=jax.ShapeDtypeStruct((width, total), jnp.bfloat16),
        grid=(bounds[-1] + 1,),
        in_specs=[pl.BlockSpec((rows, width), whole) for _ in pairs]
        + [
            pl.BlockSpec(
                (rows, block),
                functools.partial(right_index, bounds[i], bounds[i + 1] - bounds[i]),
            )
            for i in range(len(pairs))
        ]
        + [pl.BlockSpec((width, LANES), whole)],
        out_specs=pl.BlockSpec((width, block), lambda step: (0, step)),
        cost_estimate=pl.CostEstimate(
            flops=2 * rows * width * total, bytes_accessed=2 * width * total, transcendentals=0
        ),
    )(*[left for left, _ in pairs], *[right for _, right in pairs], gain_columns)


def local(hidden, cotangent, w_qkv, w_proj, w_inner, w_down, norm1_gain, norm2_gain):
    token_rows = hidden.shape[1]
    score_scale = HEAD_DIM ** (-0.5)
    gains = jnp.pad(jnp.stack([norm1_gain, norm2_gain], axis=1), ((0, 0), (0, LANES - 2)))
    packed = lax.all_gather(
        jnp.concatenate([w_qkv, w_proj, w_inner, w_down, gains], axis=1), EVERY, axis=0, tiled=True
    )
    edges = [0]
    for part in (w_qkv, w_proj, w_inner, w_down, gains):
        edges.append(edges[-1] + part.shape[1])
    full_qkv, full_proj, full_inner, full_down, full_gains = (
        packed[:, edges[i] : edges[i + 1]] for i in range(5)
    )
    first_norm_gain = full_gains[:, 0].astype(jnp.float32)
    second_norm_gain = full_gains[:, 1].astype(jnp.float32)
    input_tokens = hidden[0].astype(jnp.float32)
    first_normed_rows, first_centered_rows, first_inverse_deviation = apply_layer_norm(
        input_tokens, first_norm_gain
    )
    h_one = first_normed_rows.astype(jnp.bfloat16)
    projected = jnp.dot(h_one, full_qkv, preferred_element_type=jnp.float32)
    cosine, sine_table = rope_tables(lax.axis_index("ctx") * token_rows, token_rows, HEAD_DIM)
    query_rot = rotate(as_heads(projected[:, :D]), cosine, sine_table, 1.0).astype(jnp.bfloat16)
    key_flat = (
        rotate(as_heads(projected[:, D : 2 * D]), cosine, sine_table, 1.0)
        .astype(jnp.bfloat16)
        .reshape(token_rows, D)
    )
    value_flat = projected[:, 2 * D :].astype(jnp.bfloat16)
    key_value = lax.all_gather(
        jnp.concatenate([key_flat, value_flat], axis=1), "ctx", axis=0, tiled=True
    )
    key_whole = as_heads(key_value[:, :D])
    value_whole = as_heads(key_value[:, D:])
    scores = (
        jnp.einsum("qhd,khd->hqk", query_rot, key_whole, preferred_element_type=jnp.float32)
        * score_scale
    )
    row_peak = jnp.max(scores, axis=-1)
    weights = jnp.exp(scores - row_peak[..., None])
    row_total = jnp.sum(weights, axis=-1)
    mixture = jnp.einsum(
        "hqk,khd->qhd",
        weights.astype(jnp.bfloat16),
        value_whole,
        preferred_element_type=jnp.float32,
    )
    attended = (
        (mixture / jnp.transpose(row_total)[:, :, None])
        .reshape(token_rows, D)
        .astype(jnp.bfloat16)
    )
    residual_stream = input_tokens + jnp.dot(
        attended, full_proj, preferred_element_type=jnp.float32
    )
    second_normed_rows, second_centered_rows, second_inverse_deviation = apply_layer_norm(
        residual_stream, second_norm_gain
    )
    h_two = second_normed_rows.astype(jnp.bfloat16)
    inner_all = jnp.dot(h_two, full_inner, preferred_element_type=jnp.float32)
    act_half = inner_all[:, :FF]
    gate_half = inner_all[:, FF:]
    activated, gelu_slope = gelu_parts(act_half)
    middle = (activated * gate_half).astype(jnp.bfloat16)
    output_rows = residual_stream + jnp.einsum(
        "tf,df->td", middle, full_down, preferred_element_type=jnp.float32
    )
    upstream = cotangent[0]
    d_middle = jnp.dot(upstream, full_down, preferred_element_type=jnp.float32)
    d_inner = jnp.concatenate(
        [d_middle * gate_half * gelu_slope, d_middle * activated], axis=-1
    ).astype(jnp.bfloat16)
    second_hidden_gradient = jnp.einsum(
        "te,de->td", d_inner, full_inner, preferred_element_type=jnp.float32
    )
    residual_norm_gradient, second_gain_portion = layer_norm_gradient(
        second_hidden_gradient, second_norm_gain, second_centered_rows, second_inverse_deviation
    )
    d_resid = upstream.astype(jnp.float32) + residual_norm_gradient
    d_resid_low = d_resid.astype(jnp.bfloat16)
    d_attended = jnp.einsum(
        "td,ed->te", d_resid_low, full_proj, preferred_element_type=jnp.float32
    ).astype(jnp.bfloat16)
    grad_heads = as_heads(d_attended)
    row_delta = jnp.transpose(
        jnp.sum(grad_heads.astype(jnp.float32) * as_heads(attended).astype(jnp.float32), axis=-1)
    )
    probabilities = weights * (1.0 / row_total)[..., None]
    grad_dots = jnp.einsum(
        "qhd,khd->hqk", grad_heads, value_whole, preferred_element_type=jnp.float32
    )
    dscore = (probabilities * (grad_dots - row_delta[..., None])).astype(jnp.bfloat16)
    probs_low = probabilities.astype(jnp.bfloat16)
    key_terms = (
        jnp.einsum("hqk,qhd->khd", dscore, query_rot, preferred_element_type=jnp.float32)
        * score_scale
    )
    value_terms = jnp.einsum(
        "hqk,qhd->khd", probs_low, grad_heads, preferred_element_type=jnp.float32
    )
    whole_rows = key_value.shape[0]
    key_value_sum = lax.psum_scatter(
        jnp.concatenate(
            [
                key_terms.reshape(whole_rows, D).astype(jnp.bfloat16),
                value_terms.reshape(whole_rows, D).astype(jnp.bfloat16),
            ],
            axis=1,
        ),
        "ctx",
        scatter_dimension=0,
        tiled=True,
    )
    query_grad = (
        jnp.einsum("hqk,khd->qhd", dscore, key_whole, preferred_element_type=jnp.float32)
        * score_scale
    )
    d_query = rotate(query_grad, cosine, sine_table, -1.0)
    d_key = rotate(as_heads(key_value_sum[:, :D].astype(jnp.float32)), cosine, sine_table, -1.0)
    d_projected = jnp.concatenate(
        [
            d_query.reshape(token_rows, D).astype(jnp.bfloat16),
            d_key.reshape(token_rows, D).astype(jnp.bfloat16),
            key_value_sum[:, D:],
        ],
        axis=-1,
    )
    first_hidden_gradient = jnp.einsum(
        "te,de->td", d_projected, full_qkv, preferred_element_type=jnp.float32
    )
    input_norm_gradient, first_gain_portion = layer_norm_gradient(
        first_hidden_gradient, first_norm_gain, first_centered_rows, first_inverse_deviation
    )
    input_grad = d_resid + input_norm_gradient
    gain_columns = jnp.pad(
        jnp.stack([first_gain_portion, second_gain_portion], axis=1), ((0, 0), (0, LANES - 2))
    )
    grad_terms = weight_grads(
        [(h_one, d_projected), (attended, d_resid_low), (h_two, d_inner), (upstream, middle)],
        gain_columns,
    )
    grad_share = lax.psum_scatter(
        grad_terms, EVERY, scatter_dimension=0, tiled=True
    ).astype(jnp.float32)
    return (
        output_rows.astype(jnp.bfloat16)[None],
        input_grad[None],
        grad_share[:, edges[0] : edges[1]],
        grad_share[:, edges[1] : edges[2]],
        grad_share[:, edges[2] : edges[3]],
        grad_share[:, edges[3] : edges[4]],
        grad_share[:, edges[4]],
        grad_share[:, edges[4] + 1],
    )


def solution(mesh):
    placed = (
        P("batch", "ctx", None),
        P("batch", "ctx", None),
        P(("batch", "ctx"), None),
        P(("batch", "ctx"), None),
        P(("batch", "ctx"), None),
        P(("batch", "ctx"), None),
        P(("batch", "ctx")),
        P(("batch", "ctx")),
    )
    return jax.shard_map(
        local,
        mesh=mesh,
        in_specs=placed,
        out_specs=(
            P("batch", "ctx", None),
            P("batch", "ctx", None),
            P(("batch", "ctx"), None),
            P(("batch", "ctx"), None),
            P(("batch", "ctx"), None),
            P(("batch", "ctx"), None),
            P(("batch", "ctx")),
            P(("batch", "ctx")),
        ),
        check_vma=False,
    )
```

time: 642 us -> 394 us (0.61)
  waiting for transfers between devices: 439 us -> 288 us
  blocking collectives: 72.5 us -> 0 us
  matrix products: 62.9 us -> 28.4 us
  Pallas kernels: 0 us -> 14.5 us
  local copies, waits for them, and re-layouts: 43 us -> 29.3 us
  other arithmetic: 8.55 us -> 17.7 us
    all_gather x8 -> x2, waiting for transfers between devices: 227 us -> 122 us  [the longest x1 84.9 us: local(): lax.all_gather(jnp.concatenate([w_qkv, w_proj, w_inner, w_down, gains], a...]
    reduce_scatter x1 -> x2, waiting for transfers between devices: 210 us -> 166 us  [the longest x1 135 us: local(): lax.psum_scatter(grad_terms, EVERY, scatter_dimension=0, tiled=True)]
    unnamed x1 -> x0, blocking collectives: 42.2 us -> none
    dot_general x14 -> x10, matrix products: 52.9 us -> 21.8 us  [the longest x1 5.76 us: local(): jnp.einsum('hqk,qhd->khd', probs_low, grad_heads, preferred_element_type=...]
    all_gather x2 -> x0, blocking collectives: 30.3 us -> none  [the longest x1 15.2 us: local(): lax.all_gather(row_delta, 'ctx', axis=1, tiled=True)]
    concatenate x1, local copies, waits for them, and re-layouts: 22.2 us -> 0.01 us  [local(): jnp.concatenate([w_qkv, w_proj, w_inner, w_down, gains], axis=1)]
    pallas_call x0 -> x1, Pallas kernels: none -> 14.5 us  [weight_grads(): pl.pallas_call(functools.partial(weight_grad_kernel, tuple(bounds)), out_...]
  transfers between devices with their start and end apart: 9 -> 4, of which waited for: 7 -> 4; matrix products, arithmetic and copies ran while one was open for 8% -> 4% of each run, Pallas kernels for 0% -> 0%
where the time goes in v1:
time: 394 us; the launch traced here: 393 us
  waiting for transfers between devices  288 us (73%)
  local copies, waits for them, and re-layouts  29.3 us (7%)
  matrix products  28.4 us (7%)
  other arithmetic  17.7 us (4%)
  Pallas kernels  14.5 us (4%)
  between operations  14.4 us (4%)
    reduce_scatter x1, waiting for transfers between devices, local(): lax.psum_scatter(grad_terms, EVERY, scatter_dimension=0, tiled=True)  135 us
    all_gather x1, waiting for transfers between devices, local(): lax.all_gather(jnp.concatenate([w_qkv, w_proj, w_inner, w_down, gains], a...  84.9 us
    all_gather x1, waiting for transfers between devices, local(): lax.all_gather(jnp.concatenate([key_flat, value_flat], axis=1), 'ctx', ax...  36.9 us
    reduce_scatter x1, waiting for transfers between devices, local(): lax.psum_scatter(jnp.concatenate([key_terms.reshape(whole_rows, D).astype...  31.7 us
    pallas_call x1, Pallas kernels, weight_grads(): pl.pallas_call(functools.partial(weight_grad_kernel, tuple(bounds)), out_...  14.5 us
    unnamed x85, local copies, waits for them, and re-layouts  9.97 us
  transfers between devices with their start and end apart: 4, of which 4 were waited for; matrix products, arithmetic and copies ran while one was open for 4% of the time, Pallas kernels for 0%

profile of v1, /device:TPU:0, one launch (start us, length us, event | category | flops | bytes accessed | tf_op | source)
XLA Modules:
  0.0 392.9 jit_solution(6042153293724463607)
XLA Ops:
  7.2 0.7 pad_maximum_fusion.11
  8.0 0.9 constant_dynamic-update-slice_fusion.4
  8.9 0.8 constant_dynamic-update-slice_fusion.3
  9.7 0.9 constant_dynamic-update-slice_fusion.2
  10.6 0.8 constant_dynamic-update-slice_fusion.1
  11.4 0.7 copy-done.19
  12.2 1.0 convert_reduce_fusion
  13.3 1.1 fusion.58
  14.5 0.8 broadcast_multiply_fusion
  15.2 84.9 %all-gather.3.cloned.1.call-done = bf16[768,6656]{1,0:T(8,128)(2,1)} async-done(((bf16[24,6656]{1,0:T(8,128)(2,1)}), bf16[768,6656]{1,0:T(8,128)(2,1)}) %all-gather.3.cloned.1.call-update) | async-done | bytes 10223632 | tf_op jit(solution)/shard_map/all_gather | solution.py:134
  100.1 1.9 convert_reduce_fusion.1
  102.0 1.1 fusion.51.refs_0_
  103.1 2.7 fusion.10
  106.0 0.2 copy.55
  106.1 0.2 copy.52
  106.6 0.8 pad_maximum_fusion.3
  107.5 36.9 %all-gather.5.cloned.1.call-done = bf16[1024,1536]{1,0:T(8,128)(2,1)} async-done(((bf16[128,1536]{1,0:T(8,128)(2,1)}), bf16[1024,1536]{1,0:T(8,128)(2,1)}) %all-gather.5.cloned.1.call-update) | async-done | bytes 3145744 | tf_op jit(solution)/shard_map/all_gather | solution.py:159
  144.4 3.2 fusion.66
  147.6 0.7 copy.56
  148.4 2.3 copy.54
  150.7 1.1 multiply_reduce_fusion
  151.8 1.3 fusion.12
  153.2 1.9 copy-done
  155.0 1.4 fusion.33
  156.4 0.5 slice-done.3
  157.0 0.6 slice-done.4
  157.6 0.4 fusion.69
  158.1 0.2 multiply_reduce_fusion.4
  158.4 0.6 fusion.6
  159.1 1.4 fusion.43
  160.5 1.9 multiply_reduce_fusion.1
  162.4 0.9 fusion.65
  163.3 0.5 convolution_convert_fusion
  163.9 0.2 copy.58
  164.1 5.8 %fusion.13 = bf16[12,64,1024]{2,1,0:T(8,128)(2,1)} fusion(bf16[128,12,64]{0,2,1:T(8,128)(2,1)S(1)} %bitcast.99, f32[12,128]{1,0:T(8,128)S(1)} %broadcast_divide_fusion, f32[12,128]{1,0:T(8,128)S(1)} %copy-done.26, f32[12,128,1024]{2,1,0:T(8,128)} %copy-done), kind=kOutput, calls=%fused_computation.20 | convolution fusion | flops 208404480 | bytes 8073216 | tf_op jit(solution)/shard_map/hqk,qhd->khd/dot_general | solution.py:227
  170.0 2.4 multiply_convert_fusion
  172.3 1.6 copy-done.1
  174.0 0.6 multiply_convert_fusion.3
  174.6 0.7 copy.59
  175.3 1.7 copy.60
  177.0 2.0 pad_maximum_fusion
  179.0 0.2 reduce-scatter.5.cloned.1.call-start
  179.2 1.9 copy.65.refs_1_
  181.1 1.3 stack.22
  182.5 3.4 fusion.23
  185.8 0.9 pad_maximum_fusion.1.refs_6_
  186.7 31.7 %reduce-scatter.3.cloned.1.call-done = bf16[128,1536]{1,0:T(8,128)(2,1)} async-done(((bf16[1024,1536]{1,0:T(8,128)(2,1)}), bf16[128,1536]{1,0:T(8,128)(2,1)}) %reduce-scatter.3.cloned.1.call-update) | async-done | bytes 393232 | tf_op jit(solution)/shard_map/reduce_scatter | solution.py:231
  218.4 1.1 slice_convert_fusion.1
  219.5 0.2 copy.61
  219.7 0.8 subtract_convert_fusion.1
  220.9 0.9 pad_maximum_fusion.2.refs_4_
  221.7 3.4 fusion.57
  225.2 0.2 copy.64
  225.4 0.8 pad.9.refs_8_
  226.2 14.5 %shard_map.143 = bf16[768,6656]{1,0:T(8,128)(2,1)} custom-call(bf16[128,768]{1,0:T(8,128)(2,1)} %copy-done.8, bf16[128,768]{1,0:T(8,128)(2,1)} %copy.65.refs_1_, bf16[128,768]{1,0:T(8,128)(2,1)} %copy-done.9, bf16[128,768]{1,0:T(8,128)(2,1)} %bitcast.109, bf16[128,2304]{1,0:T(8,128)(2,1)} %pad_maximum_fusion.2.refs_4_, bf16[128,768]{1,0:T(8,128)(2,1)} %copy-done.18, ...), custom_call_target="tpu_custom_call" | custom-call | flops 1308622848 | bytes 10223616 | tf_op jit(solution)/shard_map/pallas_call | solution.py:110
  240.7 0.9 copy-done.20
  241.6 2.8 fusion.27
  244.4 0.9 fusion.56
  245.4 134.7 %reduce-scatter.5.cloned.1.call-done = bf16[24,6656]{1,0:T(8,128)(2,1)} async-done(((bf16[768,6656]{1,0:T(8,128)(2,1)}), bf16[24,6656]{1,0:T(8,128)(2,1)}) %reduce-scatter.5.cloned.1.call-update) | async-done | bytes 319504 | tf_op jit(solution)/shard_map/reduce_scatter | solution.py:271
  380.0 1.0 convert_element_type.154
  381.0 0.7 slice_reduce_fusion
  381.7 1.4 slice.144
  383.1 1.5 slice.146
  384.6 1.7 fusion.68
  (108 shorter events, 1.4 us)
Async XLA Ops:
  7.2 92.9 %all-gather.3.cloned.1.call-start = ((), (), s32[]{:S(2)}) async-start(), calls=%async_computation.2 | async-start | bytes 10543104 | tf_op jit(solution)/shard_map/all_gather | solution.py:134
  11.4 0.7 copy-start.19
  12.2 132.2 %all-gather.5.cloned.1.call-start = ((), (), s32[]{:S(2)}) async-start(), calls=%async_computation.3 | async-start | bytes 3538944 | tf_op jit(solution)/shard_map/all_gather | solution.py:159
  13.3 92.6 %copy-start.31 = (f32[128]{0:T(128)}, f32[128]{0:T(128)S(1)}, u32[]{:S(2)}) copy-start(f32[128]{0:T(128)S(1)} %broadcast_multiply_fusion.6) | copy-start | bytes 1540
  14.4 91.5 %copy-start.33 = (f32[128]{0:T(128)}, f32[128]{0:T(128)S(1)}, u32[]{:S(2)}) copy-start(f32[128]{0:T(128)S(1)} %add_rsqrt_fusion.1) | copy-start | bytes 1540
  102.0 4.0 %copy-start.27 = (f32[768]{0:T(1024)}, f32[768]{0:T(1024)S(1)}, u32[]{:S(2)}) copy-start(f32[768]{0:T(1024)S(1)} %get-tuple-element.9) | copy-start | bytes 9220
  103.1 2.9 copy-start.8
  106.4 44.2 %copy-start.13 = (bf16[128,12,32]{0,2,1:T(8,128)(2,1)}, bf16[128,12,32]{0,2,1:T(8,128)(2,1)S(1)}, u32[]{:S(2)}) copy-start(bf16[128,12,32]{0,2,1:T(8,128)(2,1)S(1)} %get-tuple-element.31) | copy-start | bytes 294916
  106.4 44.2 %copy-start.15 = (bf16[128,12,32]{0,2,1:T(8,128)(2,1)}, bf16[128,12,32]{0,2,1:T(8,128)(2,1)S(1)}, u32[]{:S(2)}) copy-start(bf16[128,12,32]{0,2,1:T(8,128)(2,1)S(1)} %get-tuple-element.32) | copy-start | bytes 294916
  107.4 111.0 %reduce-scatter.3.cloned.1.call-start = ((), (), s32[]{:S(2)}) async-start(), calls=%async_computation.4 | async-start | bytes 3538944 | tf_op jit(solution)/shard_map/reduce_scatter | solution.py:231
  148.3 3.5 copy-start.3
  150.6 2.5 copy-start.4
  150.7 5.8 %slice-start.2 = ((s8[10223616]{0:T(1024)(128)(4,1)}), s8[4194304]{0:T(1024)(128)(4,1)S(1)}, s32[]{:S(2)}) async-start(s8[10223616]{0:T(1024)(128)(4,1)} %bitcast.92), calls=%async_computation.8 | async-start | bytes 8388608
  150.7 6.3 %slice-start.3 = ((s8[10223616]{0:T(1024)(128)(4,1)}), s8[4194304]{0:T(1024)(128)(4,1)S(1)}, s32[]{:S(2)}) async-start(s8[10223616]{0:T(1024)(128)(4,1)} %bitcast.92), calls=%async_computation.9 | async-start | bytes 8388608
  151.8 3.2 copy-start
  151.8 3.2 copy-start.25
  155.0 2.6 slice-start.4
  155.0 2.6 copy-start.6
  155.0 3.2 copy-start.29
  156.4 7.6 %copy-start.10 = (bf16[128,12,64]{0,2,1:T(8,128)(2,1)}, bf16[128,12,64]{0,2,1:T(8,128)(2,1)S(1)}, u32[]{:S(2)}) copy-start(bf16[128,12,64]{0,2,1:T(8,128)(2,1)S(1)} %fusion.33) | copy-start | bytes 589828
  158.1 1.0 copy-start.17
  158.4 2.1 copy-start.9
  160.5 1.9 copy-start.21
  160.5 1.9 copy-start.23
  162.4 1.7 copy-start.26
  162.4 7.5 %slice-start = ((s8[6291456]{0:T(1024)(128)(4,1)}), s8[2097152]{0:T(1024)(128)(4,1)S(1)}, s32[]{:S(2)}) async-start(s8[6291456]{0:T(1024)(128)(4,1)} %bitcast.88), calls=%async_computation.6 | async-start | bytes 4194304
  163.3 6.6 %copy-start.18 = (bf16[128,768]{1,0:T(8,128)(2,1)}, bf16[128,768]{1,0:T(8,128)(2,1)S(1)}, u32[]{:S(2)}) copy-start(bf16[128,768]{1,0:T(8,128)(2,1)S(1)} %get-tuple-element.18.refs_5_) | copy-start | bytes 589828
  164.1 5.8 %slice-start.1 = ((s8[6291456]{0:T(1024)(128)(4,1)}), s8[4194304]{0:T(1024)(128)(4,1)S(1)}, s32[]{:S(2)}) async-start(s8[6291456]{0:T(1024)(128)(4,1)} %bitcast.88), calls=%async_computation.7 | async-start | bytes 8388608
  164.1 5.8 %copy-start.5 = (bf16[1024,768]{0,1:T(8,128)(2,1)S(1)}, bf16[1024,768]{0,1:T(8,128)(2,1)}, u32[]{:S(2)}) copy-start(bf16[1024,768]{0,1:T(8,128)(2,1)} %copy-done.4) | copy-start | bytes 4718596
  169.9 4.0 %copy-start.14 = (bf16[128,12,32]{0,2,1:T(8,128)(2,1)S(1)}, bf16[128,12,32]{0,2,1:T(8,128)(2,1)}, u32[]{:S(2)}) copy-start(bf16[128,12,32]{0,2,1:T(8,128)(2,1)} %copy-done.13) | copy-start | bytes 294916
  169.9 4.0 %copy-start.16 = (bf16[128,12,32]{0,2,1:T(8,128)(2,1)S(1)}, bf16[128,12,32]{0,2,1:T(8,128)(2,1)}, u32[]{:S(2)}) copy-start(bf16[128,12,32]{0,2,1:T(8,128)(2,1)} %copy-done.15) | copy-start | bytes 294916
  172.3 1.6 copy-start.1
  179.0 3.5 copy-start.2
  179.0 201.0 %reduce-scatter.5.cloned.1.call-start = ((), (), s32[]{:S(2)}) async-start(), calls=%async_computation.5 | async-start | bytes 10543104 | tf_op jit(solution)/shard_map/reduce_scatter | solution.py:271
  181.1 4.7 %copy-start.22 = (bf16[128,1152]{1,0:T(8,128)(2,1)S(1)}, bf16[128,1152]{1,0:T(8,128)(2,1)}, u32[]{:S(2)}) copy-start(bf16[128,1152]{1,0:T(8,128)(2,1)} %copy-done.21) | copy-start | bytes 884740
  181.1 4.7 %copy-start.24 = (bf16[128,1152]{1,0:T(8,128)(2,1)S(1)}, bf16[128,1152]{1,0:T(8,128)(2,1)}, u32[]{:S(2)}) copy-start(bf16[128,1152]{1,0:T(8,128)(2,1)} %copy-done.23) | copy-start | bytes 884740
  185.8 33.8 %copy-start.11 = (f32[128,12,64]{0,2,1:T(8,128)S(1)}, f32[128,12,64]{0,2,1:T(8,128)}, u32[]{:S(2)}) copy-start(f32[128,12,64]{0,2,1:T(8,128)} %fusion.23) | copy-start | bytes 1179652
  186.7 35.0 %copy-start.7 = (bf16[1,128,768]{2,1,0:T(8,128)(2,1)S(1)}, bf16[1,128,768]{2,1,0:T(8,128)(2,1)}, u32[]{:S(2)}) copy-start(bf16[1,128,768]{2,1,0:T(8,128)(2,1)} %param.8) | copy-start | bytes 589828
  186.7 35.0 %copy-start.28 = (f32[768]{0:T(1024)S(1)}, f32[768]{0:T(1024)}, u32[]{:S(2)}) copy-start(f32[768]{0:T(1024)} %copy-done.27) | copy-start | bytes 9220
  186.7 35.0 %copy-start.32 = (f32[128]{0:T(128)S(1)}, f32[128]{0:T(128)}, u32[]{:S(2)}) copy-start(f32[128]{0:T(128)} %copy-done.31) | copy-start | bytes 1540
  186.7 35.0 %copy-start.34 = (f32[128]{0:T(128)S(1)}, f32[128]{0:T(128)}, u32[]{:S(2)}) copy-start(f32[128]{0:T(128)} %copy-done.33) | copy-start | bytes 1540
  221.7 3.4 copy-start.30
  240.7 1.0 copy-start.20
  240.7 3.8 copy-start.12
Sparse Core Ops, SparseCore 0:
  12.3 87.7 all-gather.2
  107.5 36.7 all-gather.4
  179.1 39.2 reduce-scatter.2
  240.8 139.1 reduce-scatter.4
